TPU v7x, 256 devices: a whole 4x4x8 slice. The times are simulated.
256 devices in a mesh: sector: 8 (over x, core), section: 32 (over z, y).
Axes of the slice: x: 4, y: 4, z: 8, core: 2. Of those that a mesh axis runs over, the one named last changes fastest.
Arguments:
- vectors: bfloat16 [98304, 512], P(('sector', 'section')), may hold values from -6 to 6
- sectors: int32 [98304, 2], P(('sector', 'section')), may hold values from 0 to 31, all different within a row; in each aligned block of 384 rows (0 to 383, 384 to 767, ...) at most 36 rows name the same one
- outcomes: int32 [98304, 2], P(('sector', 'section')), may hold values from 0 to 3
- sites: bfloat16 [2, 32, 512, 2048], P(None, 'sector'), may hold values from -0.25 to 0.25
- environments: bfloat16 [2, 32, 4, 512, 512], P(None, 'sector', None, 'section'), may hold values from -100 to 150, as said below
Outputs:
- probabilities: bfloat16 [98304, 8], P(('sector', 'section'))
- final_vectors: bfloat16 [98304, 512], P(('sector', 'section'))
Inputs may be any that keep to these rules, and one draw needn't show every extreme that they name: `sectors`: in the rows of one device no sector appears more than 36 times over all orbitals together, and on some device some sector appears exactly 36 times. Every block environments[k, q, s] is symmetric and positive definite.
All inputs are finite; a program needn't handle non-finite values.
Results may differ from a plain program's by a relative error of at most 0.0049.
Values may be sent and summed in bfloat16 or wider, within the bound.
No kernel may reach another device: no remote copies, remote signals or barrier semaphores. Data moves between devices by JAX's collectives and lax.ppermute only.
A program may use at most 128 MiB of HBM per device.

v0:
```python
import jax
import jax.numpy as jnp
from jax import lax
from jax.sharding import PartitionSpec as P

OUTCOMES = 4
ORBITALS = 2


def slot_positions(labels, sector_total):
    onehot = (labels[:, None] == jnp.arange(sector_total, dtype=jnp.int32)[None, :]).astype(
        jnp.int32
    )
    before = jnp.cumsum(onehot, axis=0) - onehot
    return jnp.sum(before * onehot, axis=1)


def branch_results(amplitudes, images, id_grid, block_width):
    weights = jnp.sum(images * amplitudes, axis=-1)
    norm_sum = jnp.sum(weights, axis=-1)
    filled = id_grid >= 0.0
    branch_probs = (weights / jnp.where(filled, norm_sum, 1.0)[..., None]).astype(jnp.bfloat16)
    chosen_mask = (id_grid[..., None] == jnp.arange(OUTCOMES, dtype=jnp.float32)).astype(
        jnp.float32
    )
    chosen_weight = jnp.sum(chosen_mask * weights, axis=-1)
    picked = jnp.sum(chosen_mask[..., None] * amplitudes, axis=-2)
    rescale = lax.rsqrt(jnp.where(filled, chosen_weight, 1.0) / block_width)
    advanced = (picked * rescale[..., None]).astype(jnp.bfloat16)
    return (branch_probs, advanced)


def local(vectors, sectors, outcomes, sites, environments):
    sector_count = lax.axis_size("sector")
    per_device = sites.shape[1]
    sector_total = per_device * sector_count
    sample_count = vectors.shape[0]
    block_width = vectors.shape[1]
    capacity = max(2, (3 * sample_count + sector_total - 1) // sector_total)
    current = vectors
    columns = []
    for orbital in range(ORBITALS):
        environ_k = lax.all_gather(environments[orbital], "section", axis=2, tiled=True)
        site_k = sites[orbital]
        labels = sectors[:, orbital]
        slot_of = labels * capacity + slot_positions(labels, sector_total)
        send_rows = (
            jnp.zeros((sector_total * capacity, block_width), jnp.bfloat16).at[slot_of].set(current)
        )
        send_rows = send_rows.reshape(sector_total, capacity, block_width)
        send_ids = (
            jnp.full((sector_total * capacity,), -1.0, jnp.bfloat16)
            .at[slot_of]
            .set(outcomes[:, orbital].astype(jnp.bfloat16))
        )
        send_ids = send_ids.reshape(sector_total, capacity)
        rows_in = lax.all_to_all(send_rows, "sector", split_axis=0, concat_axis=0, tiled=True)
        ids_in = lax.all_to_all(send_ids, "sector", split_axis=0, concat_axis=0, tiled=True)
        slot_count = rows_in.shape[1]
        arranged = rows_in.reshape(sector_count, per_device, slot_count, block_width)
        amplitudes = jnp.einsum(
            "iqcb,qbf->iqcf", arranged, site_k, preferred_element_type=jnp.float32
        )
        amplitudes = amplitudes.reshape(sector_count, per_device, slot_count, OUTCOMES, block_width)
        rounded = amplitudes.astype(jnp.bfloat16)
        images = jnp.einsum(
            "iqcsb,qsbe->iqcse", rounded, environ_k, preferred_element_type=jnp.float32
        )
        id_grid = ids_in.astype(jnp.float32).reshape(sector_count, per_device, slot_count)
        branch_probs, advanced = branch_results(amplitudes, images, id_grid, block_width)
        probs_back, rows_back = (
            lax.all_to_all(
                branch_probs.reshape(sector_total, slot_count, OUTCOMES),
                "sector",
                split_axis=0,
                concat_axis=0,
                tiled=True,
            ),
            lax.all_to_all(
                advanced.reshape(sector_total, slot_count, block_width),
                "sector",
                split_axis=0,
                concat_axis=0,
                tiled=True,
            ),
        )
        columns.append(probs_back.reshape(sector_total * capacity, OUTCOMES)[slot_of])
        current = rows_back.reshape(sector_total * capacity, block_width)[slot_of]
    return (jnp.concatenate(columns, axis=1), current)


def solution(mesh):
    placed = (
        P(("sector", "section"), None),
        P(("sector", "section"), None),
        P(("sector", "section"), None),
        P(None, "sector", None, None),
        P(None, "sector", None, "section", None),
    )
    return jax.shard_map(
        local,
        mesh=mesh,
        in_specs=placed,
        out_specs=(P(("sector", "section"), None), P(("sector", "section"), None)),
        check_vma=False,
    )
```

profile of v0, /device:TPU:1, one launch (start us, length us, event | category | flops | bytes accessed | tf_op | source)
XLA Modules:
  0.0 290.2 jit_solution(226082622245741807)
XLA Ops:
  7.2 1.8 fusion.45
  9.1 0.7 all-gather.7.cloned.1.call-update
  9.8 0.7 slice_reduce_fusion.5
  10.6 0.9 reduce-window.14
  11.7 0.7 convert.4
  12.5 0.8 fusion.43
  13.3 3.0 %scatter_custom_fusion.1 = bf16[1152]{0:T(1024)(128)(2,1)S(1)} fusion(s32[384]{0:T(512)S(1)} %get-tuple-element.10, bf16[384]{0:T(512)(128)(2,1)S(1)} %get-tuple-element.13, bf16[]{:T(256)} %constant.25.clone.1), kind=kCustom, calls=%fused_computation.82 | custom fusion | bytes 2306 | tf_op jit(solution)/shard_map/scatter | solution.py:54
  16.3 0.7 all_to_all.31
  17.0 6.4 %all-to-all-start.1 = ((bf16[8,4,36]{2,1,0:T(4,128)(2,1)}), bf16[8,4,36]{2,1,0:T(4,128)(2,1)S(1)}, u32[]{:S(2)}, u32[]{:S(2)}) async-start(bf16[8,4,36]{2,1,0:T(4,128)(2,1)} %all_to_all.31), calls=%async_computation.1 | async-start | bytes 16384 | tf_op jit(solution)/shard_map/all_to_all | solution.py:58
  23.4 2.8 scatter_custom_fusion
  26.2 1.2 reshape.115
  28.0 4.8 %all-to-all-start = ((bf16[32,36,512]{2,1,0:T(8,128)(2,1)}), bf16[32,36,512]{2,1,0:T(8,128)(2,1)S(1)}, u32[]{:S(2)}, u32[]{:S(2)}) async-start(bf16[32,36,512]{2,1,0:T(8,128)(2,1)} %reshape.115), calls=%async_computation | async-start | bytes 2621440 | tf_op jit(solution)/shard_map/all_to_all | solution.py:57
  33.2 17.5 %all-to-all-done = bf16[32,36,512]{2,1,0:T(8,128)(2,1)S(1)} async-done(((bf16[32,36,512]{2,1,0:T(8,128)(2,1)}), bf16[32,36,512]{2,1,0:T(8,128)(2,1)S(1)}, u32[]{:S(2)}, u32[]{:S(2)}) %all-to-all-start) | async-done | bytes 1179680 | tf_op jit(solution)/shard_map/all_to_all | solution.py:57
  50.7 10.3 %fusion.12 = f32[8,4,36,2048]{3,2,0,1:T(8,128)} fusion(bf16[2,4,512,2048]{3,2,1,0:T(8,128)(2,1)} %param.8, bf16[8,4,36,512]{3,2,1,0:T(8,128)(2,1)S(1)} %bitcast.119), kind=kOutput, calls=%fused_computation.26 | convolution fusion | flops 2415919104 | bytes 19005440 | tf_op jit(solution)/shard_map/iqcb,qbf->iqcf/dot_general | solution.py:61
  60.9 12.0 %reshape.196 = f32[8,4,36,4,512]{4,3,2,0,1:T(4,128)} reshape(f32[8,4,36,2048]{3,2,0,1:T(8,128)} %fusion.12) | data formatting | bytes 18874368 | tf_op jit(solution)/shard_map/reshape | solution.py:64
  73.0 8.0 %multiply_reduce_fusion.1 = f32[8,4,36,512]{3,0,2,1:T(8,128)S(1)} fusion(f32[8,4,36,4,512]{4,3,2,0,1:T(4,128)} %reshape.196, f32[8,4,36,4]{3,0,2,1:T(8,128)S(1)} %copy.116), kind=kLoop, calls=%fused_computation.11 | loop fusion | flops 4128768 | bytes 11814912 | tf_op jit(solution)/shard_map/reduce_sum | solution.py:27
  81.0 3.5 %copy.117 = f32[8,4,36,512]{3,1,0,2:T(4,128)} copy(f32[8,4,36,512]{3,0,2,1:T(8,128)S(1)} %multiply_reduce_fusion.1) | data formatting | bytes 4718592 | tf_op jit(solution)/shard_map/reduce_sum | solution.py:27
  84.5 2.7 reduce_sum.110
  87.2 25.2 %all-gather.5.cloned.1.call-done = bf16[1,4,4,512,512]{4,3,2,1,0:T(8,128)(2,1)} async-done(((bf16[1,4,4,16,512]{4,3,2,1,0:T(8,128)(2,1)}), bf16[1,4,4,512,512]{4,3,2,1,0:T(8,128)(2,1)}) %all-gather.5.cloned.1.call-update) | async-done | bytes 8388624 | tf_op jit(solution)/shard_map/all_gather | solution.py:43
  112.3 19.2 %fusion.18 = (f32[8,4,36]{2,0,1:T(8,128)S(1)}, f32[8,4,36,4]{2,0,3,1:T(8,128)S(1)}) fusion(f32[8,4,36,4,512]{4,3,2,0,1:T(4,128)} %reshape.196, bf16[1,4,4,512,512]{4,3,2,1,0:T(8,128)(2,1)} %all-gather.5.cloned.1.call-done), kind=kOutput, calls=%fused_computation.28 | convolution fusion | flops 2422991360 | bytes 17848832 | tf_op jit(solution)/shard_map/iqcsb,qsbe->iqcse/dot_general | solution.py:66
  132.0 1.7 copy.122
  133.7 5.3 %all-to-all-start.3 = ((bf16[32,36,512]{2,1,0:T(8,128)(2,1)}), bf16[32,36,512]{2,1,0:T(8,128)(2,1)S(1)}, u32[]{:S(2)}, u32[]{:S(2)}) async-start(bf16[32,36,512]{2,1,0:T(8,128)(2,1)} %copy.122), calls=%async_computation.3 | async-start | bytes 2621440 | tf_op jit(solution)/shard_map/all_to_all | solution.py:79
  139.0 0.9 reduce-window.16
  140.3 3.0 %scatter_custom_fusion.3 = bf16[1152]{0:T(1024)(128)(2,1)S(1)} fusion(s32[384]{0:T(512)S(1)} %fusion.44, bf16[384]{0:T(512)(128)(2,1)S(1)} %get-tuple-element.12, bf16[]{:T(256)} %constant.25.clone.1), kind=kCustom, calls=%fused_computation.80 | custom fusion | bytes 2306 | tf_op jit(solution)/shard_map/scatter | solution.py:54
  143.3 0.7 all_to_all.36
  144.0 12.9 %all-to-all-done.3 = bf16[32,36,512]{2,1,0:T(8,128)(2,1)S(1)} async-done(((bf16[32,36,512]{2,1,0:T(8,128)(2,1)}), bf16[32,36,512]{2,1,0:T(8,128)(2,1)S(1)}, u32[]{:S(2)}, u32[]{:S(2)}) %all-to-all-start.3) | async-done | bytes 1179680 | tf_op jit(solution)/shard_map/all_to_all | solution.py:79
  156.9 4.1 %all-to-all-start.5 = ((bf16[8,4,36]{2,1,0:T(4,128)(2,1)}), bf16[8,4,36]{2,1,0:T(4,128)(2,1)S(1)}, u32[]{:S(2)}, u32[]{:S(2)}) async-start(bf16[8,4,36]{2,1,0:T(4,128)(2,1)} %all_to_all.36), calls=%async_computation.5 | async-start | bytes 16384 | tf_op jit(solution)/shard_map/all_to_all | solution.py:58
  161.3 4.1 %scatter_custom_fusion.2 = bf16[1152,512]{1,0:T(8,128)(2,1)S(1)} fusion(s32[384]{0:T(512)S(1)} %fusion.44, bf16[]{:T(256)} %constant.9.clone.1, bf16[1152,512]{1,0:T(8,128)(2,1)S(1)} %reshape.120, s32[1024]{0:T(1024)S(1)} %pad_clamp_fusion.1), kind=kCustom, calls=%fused_computation.36 | custom fusion | bytes 1179650 | tf_op jit(solution)/shard_map/scatter | solution.py:48
  165.4 1.2 reshape.121
  166.6 4.8 %all-to-all-start.4 = ((bf16[32,36,512]{2,1,0:T(8,128)(2,1)}), bf16[32,36,512]{2,1,0:T(8,128)(2,1)S(1)}, u32[]{:S(2)}, u32[]{:S(2)}) async-start(bf16[32,36,512]{2,1,0:T(8,128)(2,1)} %reshape.121), calls=%async_computation.4 | async-start | bytes 2621440 | tf_op jit(solution)/shard_map/all_to_all | solution.py:57
  171.9 0.7 reshape.222
  172.6 16.7 %all-to-all-done.4 = bf16[32,36,512]{2,1,0:T(8,128)(2,1)S(1)} async-done(((bf16[32,36,512]{2,1,0:T(8,128)(2,1)}), bf16[32,36,512]{2,1,0:T(8,128)(2,1)S(1)}, u32[]{:S(2)}, u32[]{:S(2)}) %all-to-all-start.4) | async-done | bytes 1179680 | tf_op jit(solution)/shard_map/all_to_all | solution.py:57
  189.3 4.3 %all-to-all-start.2 = ((bf16[8,2,288]{2,1,0:T(2,128)(2,1)}), bf16[8,2,288]{2,1,0:T(2,128)(2,1)S(1)}, u32[]{:S(2)}, u32[]{:S(2)}) async-start(bf16[8,2,288]{2,1,0:T(2,128)(2,1)} %reshape.222), calls=%async_computation.2 | async-start | bytes 24576 | tf_op jit(solution)/shard_map/all_to_all | solution.py:72
  193.6 10.3 %fusion.15 = f32[8,4,36,2048]{3,2,0,1:T(8,128)} fusion(bf16[2,4,512,2048]{3,2,1,0:T(8,128)(2,1)} %param.8, bf16[8,4,36,512]{3,2,1,0:T(8,128)(2,1)S(1)} %bitcast.118), kind=kOutput, calls=%fused_computation.27 | convolution fusion | flops 2415919104 | bytes 19005440 | tf_op jit(solution)/shard_map/iqcb,qbf->iqcf/dot_general | solution.py:61
  204.0 11.9 %reshape.197 = f32[8,4,36,4,512]{4,3,2,0,1:T(4,128)} reshape(f32[8,4,36,2048]{3,2,0,1:T(8,128)} %fusion.15) | data formatting | bytes 18874368 | tf_op jit(solution)/shard_map/reshape | solution.py:64
  215.9 19.1 %fusion.20 = (f32[8,4,36]{2,0,1:T(8,128)S(1)}, f32[8,4,36,4]{2,0,3,1:T(8,128)S(1)}) fusion(f32[8,4,36,4,512]{4,3,2,0,1:T(4,128)} %reshape.197, bf16[1,4,4,512,512]{4,3,2,1,0:T(8,128)(2,1)} %all-gather.7.cloned.1.call-done), kind=kOutput, calls=%fused_computation.30 | convolution fusion | flops 2422991360 | bytes 17848832 | tf_op jit(solution)/shard_map/iqcsb,qsbe->iqcse/dot_general | solution.py:66
  235.0 6.4 %multiply_reduce_fusion = f32[8,4,36,512]{3,0,2,1:T(8,128)S(1)} fusion(f32[8,4,36,4,512]{4,3,2,0,1:T(4,128)S(1)} %copy-done, f32[8,4,36,4]{3,0,2,1:T(8,128)S(1)} %copy.136), kind=kLoop, calls=%fused_computation.10 | loop fusion | flops 4128768 | bytes 11814912 | tf_op jit(solution)/shard_map/reduce_sum | solution.py:27
  241.6 3.5 %copy.137 = f32[8,4,36,512]{3,1,0,2:T(4,128)} copy(f32[8,4,36,512]{3,0,2,1:T(8,128)S(1)} %multiply_reduce_fusion) | data formatting | bytes 4718592 | tf_op jit(solution)/shard_map/reduce_sum | solution.py:27
  245.0 2.7 reduce_sum.116
  247.7 0.7 reshape.220
  248.5 4.8 %all-to-all-start.6 = ((bf16[8,2,288]{2,1,0:T(2,128)(2,1)}), bf16[8,2,288]{2,1,0:T(2,128)(2,1)S(1)}, u32[]{:S(2)}, u32[]{:S(2)}) async-start(bf16[8,2,288]{2,1,0:T(2,128)(2,1)} %reshape.220), calls=%async_computation.6 | async-start | bytes 24576 | tf_op jit(solution)/shard_map/all_to_all | solution.py:72
  253.5 1.7 copy.142
  255.2 2.7 all-to-all-done.6
  257.9 4.2 %all-to-all-start.7 = ((bf16[32,36,512]{2,1,0:T(8,128)(2,1)}), bf16[32,36,512]{2,1,0:T(8,128)(2,1)S(1)}, u32[]{:S(2)}, u32[]{:S(2)}) async-start(bf16[32,36,512]{2,1,0:T(8,128)(2,1)} %copy.142), calls=%async_computation.7 | async-start | bytes 2621440 | tf_op jit(solution)/shard_map/all_to_all | solution.py:79
  262.6 1.4 gather_fusion
  264.7 1.4 gather_fusion.1
  266.8 13.2 %all-to-all-done.7 = bf16[32,36,512]{2,1,0:T(8,128)(2,1)S(1)} async-done(((bf16[32,36,512]{2,1,0:T(8,128)(2,1)}), bf16[32,36,512]{2,1,0:T(8,128)(2,1)S(1)}, u32[]{:S(2)}, u32[]{:S(2)}) %all-to-all-start.7) | async-done | bytes 1179680 | tf_op jit(solution)/shard_map/all_to_all | solution.py:79
  280.3 2.6 gather_fusion.2
  (60 shorter events, 5.4 us)
Async XLA Ops:
  7.2 105.2 %all-gather.5.cloned.1.call-start = ((), (), s32[]{:S(2)}) async-start(), calls=%async_computation.8 | async-start | bytes 8650752 | tf_op jit(solution)/shard_map/all_gather | solution.py:43
  9.1 206.8 %all-gather.7.cloned.1.call-start = ((), (), s32[]{:S(2)}) async-start(), calls=%async_computation.9 | async-start | bytes 8650752 | tf_op jit(solution)/shard_map/all_gather | solution.py:43
  17.0 11.1 %all-to-all-start.1 = ((bf16[8,4,36]{2,1,0:T(4,128)(2,1)}), bf16[8,4,36]{2,1,0:T(4,128)(2,1)S(1)}, u32[]{:S(2)}, u32[]{:S(2)}) async-start(bf16[8,4,36]{2,1,0:T(4,128)(2,1)} %all_to_all.31), calls=%async_computation.1 | async-start | bytes 16384 | tf_op jit(solution)/shard_map/all_to_all | solution.py:58
  28.0 22.6 %all-to-all-start = ((bf16[32,36,512]{2,1,0:T(8,128)(2,1)}), bf16[32,36,512]{2,1,0:T(8,128)(2,1)S(1)}, u32[]{:S(2)}, u32[]{:S(2)}) async-start(bf16[32,36,512]{2,1,0:T(8,128)(2,1)} %reshape.115), calls=%async_computation | async-start | bytes 2621440 | tf_op jit(solution)/shard_map/all_to_all | solution.py:57
  131.9 8.3 %copy-start.1 = (s32[384,2]{0,1:T(2,128)S(1)}, s32[384,2]{0,1:T(2,128)}, u32[]{:S(2)}) copy-start(s32[384,2]{0,1:T(2,128)} %param.6) | copy-start | bytes 9220
  133.7 23.2 %all-to-all-start.3 = ((bf16[32,36,512]{2,1,0:T(8,128)(2,1)}), bf16[32,36,512]{2,1,0:T(8,128)(2,1)S(1)}, u32[]{:S(2)}, u32[]{:S(2)}) async-start(bf16[32,36,512]{2,1,0:T(8,128)(2,1)} %copy.122), calls=%async_computation.3 | async-start | bytes 2621440 | tf_op jit(solution)/shard_map/all_to_all | solution.py:79
  156.9 9.6 %all-to-all-start.5 = ((bf16[8,4,36]{2,1,0:T(4,128)(2,1)}), bf16[8,4,36]{2,1,0:T(4,128)(2,1)S(1)}, u32[]{:S(2)}, u32[]{:S(2)}) async-start(bf16[8,4,36]{2,1,0:T(4,128)(2,1)} %all_to_all.36), calls=%async_computation.5 | async-start | bytes 16384 | tf_op jit(solution)/shard_map/all_to_all | solution.py:58
  166.6 22.7 %all-to-all-start.4 = ((bf16[32,36,512]{2,1,0:T(8,128)(2,1)}), bf16[32,36,512]{2,1,0:T(8,128)(2,1)S(1)}, u32[]{:S(2)}, u32[]{:S(2)}) async-start(bf16[32,36,512]{2,1,0:T(8,128)(2,1)} %reshape.121), calls=%async_computation.4 | async-start | bytes 2621440 | tf_op jit(solution)/shard_map/all_to_all | solution.py:57
  189.3 59.2 %all-to-all-start.2 = ((bf16[8,2,288]{2,1,0:T(2,128)(2,1)}), bf16[8,2,288]{2,1,0:T(2,128)(2,1)S(1)}, u32[]{:S(2)}, u32[]{:S(2)}) async-start(bf16[8,2,288]{2,1,0:T(2,128)(2,1)} %reshape.222), calls=%async_computation.2 | async-start | bytes 24576 | tf_op jit(solution)/shard_map/all_to_all | solution.py:72
  215.9 19.2 %copy-start = (f32[8,4,36,4,512]{4,3,2,0,1:T(4,128)S(1)}, f32[8,4,36,4,512]{4,3,2,0,1:T(4,128)}, u32[]{:S(2)}) copy-start(f32[8,4,36,4,512]{4,3,2,0,1:T(4,128)} %reshape.197) | copy-start | bytes 28311556
  248.5 9.5 %all-to-all-start.6 = ((bf16[8,2,288]{2,1,0:T(2,128)(2,1)}), bf16[8,2,288]{2,1,0:T(2,128)(2,1)S(1)}, u32[]{:S(2)}, u32[]{:S(2)}) async-start(bf16[8,2,288]{2,1,0:T(2,128)(2,1)} %reshape.220), calls=%async_computation.6 | async-start | bytes 24576 | tf_op jit(solution)/shard_map/all_to_all | solution.py:72
  257.9 22.1 %all-to-all-start.7 = ((bf16[32,36,512]{2,1,0:T(8,128)(2,1)}), bf16[32,36,512]{2,1,0:T(8,128)(2,1)S(1)}, u32[]{:S(2)}, u32[]{:S(2)}) async-start(bf16[32,36,512]{2,1,0:T(8,128)(2,1)} %copy.142), calls=%async_computation.7 | async-start | bytes 2621440 | tf_op jit(solution)/shard_map/all_to_all | solution.py:79
Sparse Core Ops, SparseCore 0:
  10.6 101.7 all-gather.4
  115.5 95.3 all-gather.6
where the time goes:
time: 296 us; the launch traced here: 290 us
  waiting for transfers between devices  89.5 us (30%)
  local copies, waits for them, and re-layouts  68.9 us (23%)
  matrix products  58.9 us (20%)
  starting transfers between devices  38.9 us (13%)
  other arithmetic  19.1 us (6%)
  between operations  14.8 us (5%)
    dot_general x2, matrix products, local(): jnp.einsum('iqcsb,qsbe->iqcse', rounded, environ_k, preferred_element_typ...  38.3 us
    all_to_all x2, waiting for transfers between devices, local(): lax.all_to_all(send_rows, 'sector', split_axis=0, concat_axis=0, tiled=True)  34.2 us
    all_to_all x2, waiting for transfers between devices, local(): lax.all_to_all(advanced.reshape(sector_total, slot_count, block_width), '...  26.1 us
    all_gather x2, waiting for transfers between devices, local(): lax.all_gather(environments[orbital], 'section', axis=2, tiled=True)  25.2 us
    reshape x2, local copies, waits for them, and re-layouts, local(): amplitudes.reshape(sector_count, per_device, slot_count, OUTCOMES, block_...  23.9 us
    dot_general x2, matrix products, local(): jnp.einsum('iqcb,qbf->iqcf', arranged, site_k, preferred_element_type=jnp...  20.6 us
    reduce_sum x2, other arithmetic, branch_results(): picked = jnp.sum(chosen_mask[..., None] * amplitudes, axis=-2)  14.4 us
    reduce_sum x4, local copies, waits for them, and re-layouts, branch_results(): picked = jnp.sum(chosen_mask[..., None] * amplitudes, axis=-2)  12.3 us
  transfers between devices with their start and end apart: 10, of which 7 were waited for; matrix products, arithmetic and copies ran while one was open for 49% of the time, Pallas kernels for 0%

commit v1 on v0

--- a/solution.py
+++ b/solution.py
@@ -40,7 +40,12 @@
     current = vectors
     columns = []
     for orbital in range(ORBITALS):
-        environ_k = lax.all_gather(environments[orbital], "section", axis=2, tiled=True)
+        environ_k = jnp.concatenate(
+            lax.all_to_all(
+                jnp.stack([environments[orbital]] * lax.axis_size("section")), "section", 0, 0
+            ),
+            axis=2,
+        )
         site_k = sites[orbital]
         labels = sectors[:, orbital]
         slot_of = labels * capacity + slot_positions(labels, sector_total)

time: 296 us -> 635 us (2.15)
  waiting for transfers between devices: 89.5 us -> 375 us
  local copies, waits for them, and re-layouts: 68.9 us -> 91.6 us
  blocking collectives: 0 us -> 22.5 us
  starting transfers between devices: 38.9 us -> 56.7 us
  between operations: 14.8 us -> 1.54 us
    all_to_all x0 -> x2, waiting for transfers between devices: none -> 332 us  [local(): lax.all_to_all(jnp.stack([environments[orbital]] * lax.axis_size('section...]
    all_gather x2 -> x0, waiting for transfers between devices: 25.2 us -> none  [local(): lax.all_gather(environments[orbital], 'section', axis=2, tiled=True)]
    all_to_all x0 -> x2, starting transfers between devices: none -> 22.8 us  [local(): lax.all_to_all(jnp.stack([environments[orbital]] * lax.axis_size('section...]
    all_to_all x0 -> x1, blocking collectives: none -> 22.5 us  [local(): lax.all_to_all(advanced.reshape(sector_total, slot_count, block_width), '...]
    reshape x0 -> x2, local copies, waits for them, and re-layouts: none -> 16.5 us  [local(): jnp.concatenate(lax.all_to_all(jnp.stack([environments[orbital]] * lax.ax...]
    all_to_all x2 -> x1, waiting for transfers between devices: 26.1 us -> 13.2 us  [local(): lax.all_to_all(advanced.reshape(sector_total, slot_count, block_width), '...]
    another operation x1 -> x3, local copies, waits for them, and re-layouts: 0.22 us -> 8.87 us  [the longest x2 8.65 us: local(): jnp.stack([environments[orbital]] * lax.axis_size('section'))]
    all_to_all x2, waiting for transfers between devices: 34.2 us -> 26.3 us  [local(): lax.all_to_all(send_rows, 'sector', split_axis=0, concat_axis=0, tiled=True)]
  transfers between devices with their start and end apart: 10 -> 9, of which waited for: 7 -> 7; matrix products, arithmetic and copies ran while one was open for 49% -> 24% of each run, Pallas kernels for 0% -> 0%
where the time goes in v1:
time: 635 us; the launch traced here: 625 us
  waiting for transfers between devices  375 us (59%)
  local copies, waits for them, and re-layouts  91.6 us (14%)
  matrix products  58.5 us (9%)
  starting transfers between devices  56.7 us (9%)
  blocking collectives  22.5 us (4%)
  other arithmetic  19.2 us (3%)
    all_to_all x2, waiting for transfers between devices, local(): lax.all_to_all(jnp.stack([environments[orbital]] * lax.axis_size('section...  332 us
    dot_general x2, matrix products, local(): jnp.einsum('iqcsb,qsbe->iqcse', rounded, environ_k, preferred_element_typ...  38 us
    all_to_all x2, waiting for transfers between devices, local(): lax.all_to_all(send_rows, 'sector', split_axis=0, concat_axis=0, tiled=True)  26.3 us
    reshape x2, local copies, waits for them, and re-layouts, local(): amplitudes.reshape(sector_count, per_device, slot_count, OUTCOMES, block_...  23.8 us
    all_to_all x2, starting transfers between devices, local(): lax.all_to_all(jnp.stack([environments[orbital]] * lax.axis_size('section...  22.8 us
    all_to_all x1, blocking collectives, local(): lax.all_to_all(advanced.reshape(sector_total, slot_count, block_width), '...  22.5 us
    dot_general x2, matrix products, local(): jnp.einsum('iqcb,qbf->iqcf', arranged, site_k, preferred_element_type=jnp...  20.5 us
    reshape x2, local copies, waits for them, and re-layouts, local(): jnp.concatenate(lax.all_to_all(jnp.stack([environments[orbital]] * lax.ax...  16.5 us
  transfers between devices with their start and end apart: 9, of which 7 were waited for; matrix products, arithmetic and copies ran while one was open for 24% of the time, Pallas kernels for 0%

profile of v1, /device:TPU:1, one launch (start us, length us, event | category | flops | bytes accessed | tf_op | source)
XLA Modules:
  0.0 625.0 jit_solution(16497449968998747494)
XLA Ops:
  0.6 0.8 slice_reduce_fusion.5
  1.4 0.9 reduce-window.14
  2.7 0.8 fusion.41
  4.2 3.0 scatter_custom_fusion.1
  7.1 0.7 all_to_all.38
  7.8 6.5 %all-to-all-start.2 = ((bf16[8,4,36]{2,1,0:T(4,128)(2,1)}), bf16[8,4,36]{2,1,0:T(4,128)(2,1)S(1)}, u32[]{:S(2)}, u32[]{:S(2)}) async-start(bf16[8,4,36]{2,1,0:T(4,128)(2,1)} %all_to_all.38), calls=%async_computation.2 | async-start | bytes 16384 | tf_op jit(solution)/shard_map/all_to_all | solution.py:63
  14.3 2.8 scatter_custom_fusion
  17.1 1.2 reshape.129
  19.0 4.2 all-to-all-start
  23.2 17.9 %all-to-all-done = bf16[32,36,512]{2,1,0:T(8,128)(2,1)S(1)} async-done(((bf16[32,36,512]{2,1,0:T(8,128)(2,1)}), bf16[32,36,512]{2,1,0:T(8,128)(2,1)S(1)}, u32[]{:S(2)}, u32[]{:S(2)}) %all-to-all-start) | async-done | bytes 1179680 | tf_op jit(solution)/shard_map/all_to_all | solution.py:62
  41.1 4.4 stack.6
  45.4 10.8 %all-to-all-start.1 = ((bf16[32,4,4,16,512]{4,3,2,1,0:T(8,128)(2,1)}), bf16[32,4,4,16,512]{4,3,2,1,0:T(8,128)(2,1)}, u32[]{:S(2)}, u32[]{:S(2)}) async-start(bf16[32,4,4,16,512]{4,3,2,1,0:T(8,128)(2,1)} %stack.6), calls=%async_computation.1 | async-start | bytes 16777216 | tf_op jit(solution)/shard_map/all_to_all | solution.py:44
  56.2 0.9 reduce-window.16
  57.5 3.5 scatter_custom_fusion.3
  61.0 0.7 all_to_all.44
  62.1 10.3 %fusion.10 = f32[8,4,36,2048]{3,2,0,1:T(8,128)} fusion(bf16[2,4,512,2048]{3,2,1,0:T(8,128)(2,1)} %param.8, bf16[8,4,36,512]{3,2,1,0:T(8,128)(2,1)S(1)} %bitcast.124), kind=kOutput, calls=%fused_computation.24 | convolution fusion | flops 2415919104 | bytes 19005440 | tf_op jit(solution)/shard_map/iqcb,qbf->iqcf/dot_general | solution.py:66
  72.4 11.9 %reshape.212 = f32[8,4,36,4,512]{4,3,2,0,1:T(4,128)} reshape(f32[8,4,36,2048]{3,2,0,1:T(8,128)} %fusion.10) | data formatting | bytes 18874368 | tf_op jit(solution)/shard_map/reshape | solution.py:69
  84.2 8.0 %multiply_reduce_fusion.1 = f32[8,4,36,512]{3,0,2,1:T(8,128)S(1)} fusion(f32[8,4,36,4,512]{4,3,2,0,1:T(4,128)} %reshape.212, f32[8,4,36,4]{3,0,2,1:T(8,128)S(1)} %copy.121), kind=kLoop, calls=%fused_computation.11 | loop fusion | flops 4128768 | bytes 11814912 | tf_op jit(solution)/shard_map/reduce_sum | solution.py:27
  92.2 3.5 copy.122
  95.7 2.7 reduce_sum.110
  98.4 147.3 %all-to-all-done.1 = bf16[32,4,4,16,512]{4,3,2,1,0:T(8,128)(2,1)} async-done(((bf16[32,4,4,16,512]{4,3,2,1,0:T(8,128)(2,1)}), bf16[32,4,4,16,512]{4,3,2,1,0:T(8,128)(2,1)}, u32[]{:S(2)}, u32[]{:S(2)}) %all-to-all-start.1) | async-done | bytes 8388640 | tf_op jit(solution)/shard_map/all_to_all | solution.py:44
  245.7 4.9 all-to-all-start.7
  250.6 8.2 %copy.111 = bf16[4,4,32,16,512]{4,3,2,1,0:T(8,128)(2,1)} copy(bf16[4,4,32,16,512]{4,3,1,0,2:T(8,128)(2,1)} %bitcast.7) | data formatting | bytes 16777216 | tf_op jit(solution)/shard_map/reshape | solution.py:43
  258.8 18.9 %fusion.16 = (f32[8,4,36]{2,0,1:T(8,128)S(1)}, f32[8,4,36,4]{2,0,3,1:T(8,128)S(1)}) fusion(f32[8,4,36,4,512]{4,3,2,0,1:T(4,128)} %reshape.212, bf16[4,4,512,512,1]{3,2,4,1,0:T(8,128)(2,1)} %bitcast.123), kind=kOutput, calls=%fused_computation.26 | convolution fusion | flops 2422991360 | bytes 17848832 | tf_op jit(solution)/shard_map/iqcsb,qsbe->iqcse/dot_general | solution.py:71
  278.8 22.5 %all_to_all.58 = bf16[32,36,512]{2,1,0:T(8,128)(2,1)S(1)} all-to-all(bf16[32,36,512]{2,1,0:T(8,128)(2,1)S(1)} %copy.127), channel_id=1, replica_groups=mesh['sector'=8,'section'=32] {'sector'}, dimensions={0} | all-to-all | bytes 2359296 | tf_op jit(solution)/shard_map/all_to_all | solution.py:84
  301.3 4.3 stack.7
  305.6 12.0 %all-to-all-start.6 = ((bf16[32,4,4,16,512]{4,3,2,1,0:T(8,128)(2,1)}), bf16[32,4,4,16,512]{4,3,2,1,0:T(8,128)(2,1)}, u32[]{:S(2)}, u32[]{:S(2)}) async-start(bf16[32,4,4,16,512]{4,3,2,1,0:T(8,128)(2,1)} %stack.7), calls=%async_computation.6 | async-start | bytes 16777216 | tf_op jit(solution)/shard_map/all_to_all | solution.py:44
  317.9 4.1 scatter_custom_fusion.2
  322.0 1.2 reshape.137
  323.2 184.8 %all-to-all-done.6 = bf16[32,4,4,16,512]{4,3,2,1,0:T(8,128)(2,1)} async-done(((bf16[32,4,4,16,512]{4,3,2,1,0:T(8,128)(2,1)}), bf16[32,4,4,16,512]{4,3,2,1,0:T(8,128)(2,1)}, u32[]{:S(2)}, u32[]{:S(2)}) %all-to-all-start.6) | async-done | bytes 8388640 | tf_op jit(solution)/shard_map/all_to_all | solution.py:44
  508.0 4.9 all-to-all-start.5
  513.4 8.3 %copy.131 = bf16[4,4,32,16,512]{4,3,2,1,0:T(8,128)(2,1)} copy(bf16[4,4,32,16,512]{4,3,1,0,2:T(8,128)(2,1)} %bitcast.22) | data formatting | bytes 16777216 | tf_op jit(solution)/shard_map/reshape | solution.py:43
  522.4 8.5 %all-to-all-done.5 = bf16[32,36,512]{2,1,0:T(8,128)(2,1)S(1)} async-done(((bf16[32,36,512]{2,1,0:T(8,128)(2,1)}), bf16[32,36,512]{2,1,0:T(8,128)(2,1)S(1)}, u32[]{:S(2)}, u32[]{:S(2)}) %all-to-all-start.5) | async-done | bytes 1179680 | tf_op jit(solution)/shard_map/all_to_all | solution.py:62
  530.9 4.4 all-to-all-start.3
  535.2 10.3 %fusion.13 = f32[8,4,36,2048]{3,2,0,1:T(8,128)} fusion(bf16[2,4,512,2048]{3,2,1,0:T(8,128)(2,1)} %param.8, bf16[8,4,36,512]{3,2,1,0:T(8,128)(2,1)S(1)} %bitcast.125), kind=kOutput, calls=%fused_computation.25 | convolution fusion | flops 2415919104 | bytes 19005440 | tf_op jit(solution)/shard_map/iqcb,qbf->iqcf/dot_general | solution.py:66
  545.5 11.9 %reshape.213 = f32[8,4,36,4,512]{4,3,2,0,1:T(4,128)} reshape(f32[8,4,36,2048]{3,2,0,1:T(8,128)} %fusion.13) | data formatting | bytes 18874368 | tf_op jit(solution)/shard_map/reshape | solution.py:69
  557.4 19.1 %fusion.18 = (f32[8,4,36]{2,0,1:T(8,128)S(1)}, f32[8,4,36,4]{2,0,3,1:T(8,128)S(1)}) fusion(f32[8,4,36,4,512]{4,3,2,0,1:T(4,128)} %reshape.213, bf16[4,4,512,512,1]{3,2,4,1,0:T(8,128)(2,1)} %bitcast.122), kind=kOutput, calls=%fused_computation.28 | convolution fusion | flops 2422991360 | bytes 17848832 | tf_op jit(solution)/shard_map/iqcsb,qsbe->iqcse/dot_general | solution.py:71
  576.6 6.4 %multiply_reduce_fusion = f32[8,4,36,512]{3,0,2,1:T(8,128)S(1)} fusion(f32[8,4,36,4,512]{4,3,2,0,1:T(4,128)S(1)} %bitcast.121, f32[8,4,36,4]{3,0,2,1:T(8,128)S(1)} %copy.142), kind=kLoop, calls=%fused_computation.10 | loop fusion | flops 4128768 | bytes 11814912 | tf_op jit(solution)/shard_map/reduce_sum | solution.py:27
  583.2 3.5 copy.143
  586.6 2.7 reduce_sum.116
  590.1 4.8 all-to-all-start.8
  595.1 1.7 copy.148
  596.8 2.7 all-to-all-done.8
  599.5 4.2 all-to-all-start.9
  604.2 1.4 gather_fusion
  606.2 1.4 gather_fusion.1
  608.4 13.2 %all-to-all-done.9 = bf16[32,36,512]{2,1,0:T(8,128)(2,1)S(1)} async-done(((bf16[32,36,512]{2,1,0:T(8,128)(2,1)}), bf16[32,36,512]{2,1,0:T(8,128)(2,1)S(1)}, u32[]{:S(2)}, u32[]{:S(2)}) %all-to-all-start.9) | async-done | bytes 1179680 | tf_op jit(solution)/shard_map/all_to_all | solution.py:84
  621.9 2.6 gather_fusion.2
  (68 shorter events, 8.1 us)
Async XLA Ops:
  0.6 22.5 %copy-start = (bf16[2,4,4,16,512]{4,3,2,1,0:T(8,128)(2,1)S(1)}, bf16[2,4,4,16,512]{4,3,2,1,0:T(8,128)(2,1)}, u32[]{:S(2)}) copy-start(bf16[2,4,4,16,512]{4,3,2,1,0:T(8,128)(2,1)} %param.9) | copy-start | bytes 1572868
  7.8 11.1 %all-to-all-start.2 = ((bf16[8,4,36]{2,1,0:T(4,128)(2,1)}), bf16[8,4,36]{2,1,0:T(4,128)(2,1)S(1)}, u32[]{:S(2)}, u32[]{:S(2)}) async-start(bf16[8,4,36]{2,1,0:T(4,128)(2,1)} %all_to_all.38), calls=%async_computation.2 | async-start | bytes 16384 | tf_op jit(solution)/shard_map/all_to_all | solution.py:63
  19.0 22.1 %all-to-all-start = ((bf16[32,36,512]{2,1,0:T(8,128)(2,1)}), bf16[32,36,512]{2,1,0:T(8,128)(2,1)S(1)}, u32[]{:S(2)}, u32[]{:S(2)}) async-start(bf16[32,36,512]{2,1,0:T(8,128)(2,1)} %reshape.129), calls=%async_computation | async-start | bytes 2621440 | tf_op jit(solution)/shard_map/all_to_all | solution.py:62
  45.4 12.0 %copy-start.1 = (s32[384,2]{0,1:T(2,128)S(1)}, s32[384,2]{0,1:T(2,128)}, u32[]{:S(2)}) copy-start(s32[384,2]{0,1:T(2,128)} %param.6) | copy-start | bytes 9220
  45.4 200.3 %all-to-all-start.1 = ((bf16[32,4,4,16,512]{4,3,2,1,0:T(8,128)(2,1)}), bf16[32,4,4,16,512]{4,3,2,1,0:T(8,128)(2,1)}, u32[]{:S(2)}, u32[]{:S(2)}) async-start(bf16[32,4,4,16,512]{4,3,2,1,0:T(8,128)(2,1)} %stack.6), calls=%async_computation.1 | async-start | bytes 16777216 | tf_op jit(solution)/shard_map/all_to_all | solution.py:44
  245.7 33.1 %all-to-all-start.7 = ((bf16[8,4,36]{2,1,0:T(4,128)(2,1)}), bf16[8,4,36]{2,1,0:T(4,128)(2,1)S(1)}, u32[]{:S(2)}, u32[]{:S(2)}) async-start(bf16[8,4,36]{2,1,0:T(4,128)(2,1)} %all_to_all.44), calls=%async_computation.7 | async-start | bytes 16384 | tf_op jit(solution)/shard_map/all_to_all | solution.py:63
  305.6 202.4 %all-to-all-start.6 = ((bf16[32,4,4,16,512]{4,3,2,1,0:T(8,128)(2,1)}), bf16[32,4,4,16,512]{4,3,2,1,0:T(8,128)(2,1)}, u32[]{:S(2)}, u32[]{:S(2)}) async-start(bf16[32,4,4,16,512]{4,3,2,1,0:T(8,128)(2,1)} %stack.7), calls=%async_computation.6 | async-start | bytes 16777216 | tf_op jit(solution)/shard_map/all_to_all | solution.py:44
  508.0 22.9 %all-to-all-start.5 = ((bf16[32,36,512]{2,1,0:T(8,128)(2,1)}), bf16[32,36,512]{2,1,0:T(8,128)(2,1)S(1)}, u32[]{:S(2)}, u32[]{:S(2)}) async-start(bf16[32,36,512]{2,1,0:T(8,128)(2,1)} %reshape.137), calls=%async_computation.5 | async-start | bytes 2621440 | tf_op jit(solution)/shard_map/all_to_all | solution.py:62
  530.9 59.2 %all-to-all-start.3 = ((bf16[8,2,288]{2,1,0:T(2,128)(2,1)}), bf16[8,2,288]{2,1,0:T(2,128)(2,1)S(1)}, u32[]{:S(2)}, u32[]{:S(2)}) async-start(bf16[8,2,288]{2,1,0:T(2,128)(2,1)} %reshape.238), calls=%async_computation.3 | async-start | bytes 24576 | tf_op jit(solution)/shard_map/all_to_all | solution.py:77
  557.4 19.2 %slice-start = ((s8[9437184]{0:T(1024)(128)(4,1)}), s8[4194304]{0:T(1024)(128)(4,1)S(1)}, s32[]{:S(2)}) async-start(s8[9437184]{0:T(1024)(128)(4,1)} %bitcast.120), calls=%async_computation.10 | async-start | bytes 8388608
  557.4 19.2 %slice-start.1 = ((s8[9437184]{0:T(1024)(128)(4,1)}), s8[4194304]{0:T(1024)(128)(4,1)S(1)}, s32[]{:S(2)}) async-start(s8[9437184]{0:T(1024)(128)(4,1)} %bitcast.120), calls=%async_computation.11 | async-start | bytes 8388608
  557.4 19.2 %slice-start.2 = ((s8[9437184]{0:T(1024)(128)(4,1)}), s8[1048576]{0:T(1024)(128)(4,1)S(1)}, s32[]{:S(2)}) async-start(s8[9437184]{0:T(1024)(128)(4,1)} %bitcast.120), calls=%async_computation.12 | async-start | bytes 2097152
  590.1 9.5 %all-to-all-start.8 = ((bf16[8,2,288]{2,1,0:T(2,128)(2,1)}), bf16[8,2,288]{2,1,0:T(2,128)(2,1)S(1)}, u32[]{:S(2)}, u32[]{:S(2)}) async-start(bf16[8,2,288]{2,1,0:T(2,128)(2,1)} %reshape.236), calls=%async_computation.8 | async-start | bytes 24576 | tf_op jit(solution)/shard_map/all_to_all | solution.py:77
  599.5 22.1 %all-to-all-start.9 = ((bf16[32,36,512]{2,1,0:T(8,128)(2,1)}), bf16[32,36,512]{2,1,0:T(8,128)(2,1)S(1)}, u32[]{:S(2)}, u32[]{:S(2)}) async-start(bf16[32,36,512]{2,1,0:T(8,128)(2,1)} %copy.148), calls=%async_computation.9 | async-start | bytes 2621440 | tf_op jit(solution)/shard_map/all_to_all | solution.py:84
